TPU v7x, 512 devices: a whole 4x8x8 slice. The times are simulated.
512 devices in a mesh: ty: 16 (over x_lo, z), tx: 32 (over y, x_hi, core).
Axes of the slice: x: 4 (x_hi: 2, x_lo: 2; x = x_hi * 2 + x_lo), y: 8, z: 8, core: 2. Of those that a mesh axis runs over, the one named last changes fastest.
Arguments:
- observed: float32 [6, 2048, 8192], P(None, 'ty', 'tx'), may hold values from -6 to 6
- inverse_variance: float32 [6, 2048, 8192], P(None, 'ty', 'tx'), may hold values from 0.5 to 4
- sed: float32 [16, 32, 6], P('ty', 'tx'), may hold values from 0.2 to 2
- morph: float32 [16, 32, 128, 128], P('ty', 'tx'), may hold values from 0.02 to 1
- foot_block: int32 [16, 32], P('ty', 'tx'), may hold values from 0 to 63, as said below
- gamma: float32 [16, 32], P('ty', 'tx'), may hold values from 0.3 to 1.5
- row_kernel: float32 [6, 41], replicated, may hold values from -1 to 1
- col_kernel: float32 [6, 41], replicated, may hold values from -1 to 1
Outputs:
- residual: float32 [6, 2048, 8192], P(None, 'ty', 'tx')
- new_morph: float32 [16, 32, 128, 128], P('ty', 'tx')
- new_sed: float32 [16, 32, 6], P('ty', 'tx')
Inputs may be any that keep to these rules, and one draw needn't show every extreme that they name: A source's footprint lies in its own tile row, at box column foot_block counted over the whole row; in every tile row at most 2 sources lie in one tile of 2 box columns, and some tile holds exactly 2.
All inputs are finite; a program needn't handle non-finite values.
Results may differ from a plain program's by a relative error of at most 0.0003.
Values sent between devices are 32-bit elements; how exact they have to be, the bound alone decides.
A program may use at most 64 MiB of HBM per device.

v0:
```python
import jax
import jax.numpy as jnp
from jax import lax
from jax.sharding import PartitionSpec as P

HIGHEST_PRECISION = lax.Precision.HIGHEST


def with_halo(value, sides, width):
    for axis, dim in sides:
        devices, length = (lax.axis_size(axis), value.shape[dim])
        up = [(i, (i + 1) % devices) for i in range(devices - 1)]
        down = [(j, i) for i, j in up]
        last = lax.slice_in_dim(value, length - width, length, axis=dim)
        leading = lax.slice_in_dim(value, 0, width, axis=dim)
        before = lax.ppermute(last, axis, up)
        after = lax.ppermute(leading, axis, down)
        value = jnp.concatenate([before, value, after], axis=dim)
    return value


def taps_matrix(kernel, length):
    taps_count = kernel.shape[1]
    span = length + taps_count - 1
    offset = (
        jnp.arange(span, dtype=jnp.int32)[:, None] - jnp.arange(length, dtype=jnp.int32)[None, :]
    )
    select = (offset[None] == jnp.arange(taps_count, dtype=jnp.int32)[:, None, None]).astype(
        jnp.float32
    )
    return jnp.einsum("bt,tqc->bqc", kernel, select, precision=HIGHEST_PRECISION)


def apply_columns(padded, matrix, per_tile, box_size):
    window = matrix.shape[1]
    windows = jnp.stack(
        [padded[:, :, block * box_size : block * box_size + window] for block in range(per_tile)],
        axis=2,
    )
    mixed = jnp.einsum("brjq,bqc->brjc", windows, matrix, precision=HIGHEST_PRECISION)
    return mixed.reshape(padded.shape[0], padded.shape[1], per_tile * box_size)


def body(observed, inverse_variance, sed, morph, foot_block, gamma, row_kernel, col_kernel):
    band_count, tile_rows, tile_cols = observed.shape
    box_size = morph.shape[2]
    per_tile = tile_cols // box_size
    rim_width = (row_kernel.shape[1] - 1) // 2
    all_sed, all_morph, all_foot = (
        lax.all_gather(sed, "tx", axis=1, tiled=True),
        lax.all_gather(morph, "tx", axis=1, tiled=True),
        lax.all_gather(foot_block, "tx", axis=1, tiled=True),
    )
    all_sed = all_sed[0]
    all_morph = all_morph[0]
    all_foot = all_foot[0]
    tile_index = lax.axis_index("tx")
    first_block = tile_index * per_tile
    placed = (
        all_foot[:, None] == first_block + jnp.arange(per_tile, dtype=jnp.int32)[None, :]
    ).astype(jnp.float32)
    weighted = placed[:, None, :] * all_sed[:, :, None]
    model = jnp.einsum("kbj,krc->brjc", weighted, all_morph, precision=HIGHEST_PRECISION).reshape(
        band_count, tile_rows, tile_cols
    )
    flip_rows = taps_matrix(row_kernel[:, ::-1], tile_rows)
    flip_cols = taps_matrix(col_kernel[:, ::-1], box_size)
    wide_model = with_halo(model, (("tx", 2),), rim_width)
    blurred = apply_columns(wide_model, flip_cols, per_tile, box_size)
    tall_blurred = with_halo(blurred, (("ty", 1),), rim_width)
    predicted = jnp.einsum("bqw,bqr->brw", tall_blurred, flip_rows, precision=HIGHEST_PRECISION)
    residual = inverse_variance * (observed - predicted)
    corr_rows = taps_matrix(row_kernel, tile_rows)
    corr_cols = taps_matrix(col_kernel, box_size)
    tall_resid = with_halo(residual, (("ty", 1),), rim_width)
    backrows = jnp.einsum("bqw,bqr->brw", tall_resid, corr_rows, precision=HIGHEST_PRECISION)
    wide_back = with_halo(backrows, (("tx", 2),), rim_width)
    gradient = apply_columns(wide_back, corr_cols, per_tile, box_size)
    grid = gradient.reshape(band_count, tile_rows, per_tile, box_size)
    morph_terms = jnp.einsum("kbj,brjc->krc", weighted, grid, precision=HIGHEST_PRECISION)
    raw_terms = jnp.einsum("krc,brjc->kbj", all_morph, grid, precision=HIGHEST_PRECISION)
    sed_terms = jnp.sum(raw_terms * placed[:, None, :], axis=2)
    morph_grad, sed_grad = (
        lax.psum_scatter(morph_terms, "tx", scatter_dimension=0, tiled=True),
        lax.psum_scatter(sed_terms, "tx", scatter_dimension=0, tiled=True),
    )
    own_sed = sed[0]
    own_morph = morph[0]
    own_gamma = gamma[0]
    step_morph = own_gamma / jnp.sum(own_sed * own_sed, axis=1)
    new_morph = jnp.maximum(own_morph + step_morph[:, None, None] * morph_grad, 0.0)
    step_sed = own_gamma / jnp.sqrt(jnp.sum(own_morph * own_morph, axis=(1, 2)))
    new_sed = jnp.maximum(own_sed + step_sed[:, None] * sed_grad, 0.0)
    return (residual, new_morph[None], new_sed[None])


def solution(mesh):
    in_specs = (
        P(None, "ty", "tx"),
        P(None, "ty", "tx"),
        P("ty", "tx", None),
        P("ty", "tx", None, None),
        P("ty", "tx"),
        P("ty", "tx"),
        P(),
        P(),
    )
    out_specs = (P(None, "ty", "tx"), P("ty", "tx", None, None), P("ty", "tx", None))
    return jax.shard_map(body, mesh=mesh, in_specs=in_specs, out_specs=out_specs, check_vma=False)
```

profile of v0, /device:TPU:96, one launch (start us, length us, event | category | flops | bytes accessed | tf_op | source)
XLA Modules:
  0.0 315.2 jit_solution(1384068626255635407)
XLA Ops:
  7.2 0.0 all-gather.2.cloned.1.call-start
  7.2 0.7 all-gather.2.cloned.1.call-update
  7.9 0.0 reduce-scatter.2.cloned.1.call-start
  8.6 0.8 rev.7
  9.4 39.6 %all_gather.10 = f32[1,32,6]{2,0,1:T(1,128)S(1)} all-gather(f32[1,1,6]{2,0,1:T(1,128)} %bitcast.108), channel_id=1, replica_groups=mesh['ty'=16,'tx'=32] {'tx'}, dimensions={1}, use_global_device_ids=true | all-gather | bytes 792 | tf_op jit(solution)/shard_map/all_gather | solution.py:50
  48.9 0.1 copy.32
  49.0 1.4 fusion.78
  50.4 0.7 bitcast_dynamic-update-slice_fusion
  51.1 13.8 %all-reduce = s32[32]{0:T(128)S(1)} all-reduce(s32[32]{0:T(128)S(1)} %bitcast_dynamic-update-slice_fusion), channel_id=1, replica_groups=mesh['ty'=16,'tx'=32] {'tx'}, use_global_device_ids=true, to_apply=%add | all-reduce | flops 32 | bytes 256
  64.9 0.1 compare_convert_fusion
  65.0 32.4 %all-gather.2.cloned.1.call-done = f32[1,32,128,128]{3,2,0,1:T(8,128)} async-done(((f32[1,1,128,128]{3,2,0,1:T(8,128)}), f32[1,32,128,128]{3,2,0,1:T(8,128)}) %all-gather.2.cloned.1.call-update) | async-done | bytes 2097168 | tf_op jit(solution)/shard_map/all_gather | solution.py:51
  97.4 4.0 %fusion.16 = f32[6,128,2,128]{3,0,1,2:T(8,128)S(1)} fusion(f32[1,32,128,128]{3,2,0,1:T(8,128)} %all-gather.2.cloned.1.call-done, f32[32,6]{0,1:T(8,128)S(1)} %copy.32, f32[32,2]{0,1:T(2,128)S(1)} %compare_convert_fusion), kind=kOutput, calls=%fused_computation.19 | convolution fusion | flops 75497856 | bytes 2884608 | tf_op jit(solution)/shard_map/kbj,krc->brjc/dot_general | solution.py:63
  101.4 0.0 copy-start.5
  101.4 0.3 copy.35
  101.8 2.1 collective-permute-start
  103.9 7.0 %collective-permute-start.1 = (f32[6,128,20]{1,2,0:T(8,128)S(1)}, f32[6,128,20]{1,2,0:T(8,128)S(1)}, u32[]{:S(2)}, u32[]{:S(2)}) collective-permute-start(f32[6,128,20]{1,2,0:T(8,128)S(1)} %get-tuple-element.14), channel_id=1, source_target_pairs={{1,0},{2,1},{3,2},{4,3},{5,4},{6,5},{7,6},{8,7},{9,8},{10,9},{11,1... | collective-permute-start | bytes 184328 | tf_op jit(solution)/shard_map/ppermute | solution.py:17
  111.0 1.5 fusion.21
  112.5 0.0 copy-done.5
  112.5 0.1 rev.6
  112.5 0.0 collective-permute-done
  112.5 0.4 collective-permute-done.1
  112.9 0.1 fusion.53
  113.0 1.5 fusion.35
  114.5 0.0 copy-start.2
  114.6 0.0 copy-start.3
  114.6 0.3 copy.37
  114.9 3.7 %collective-permute-start.2 = (f32[6,20,256]{2,1,0:T(8,128)S(1)}, f32[6,20,256]{2,1,0:T(8,128)S(1)}, u32[]{:S(2)}, u32[]{:S(2)}) collective-permute-start(f32[6,20,256]{2,1,0:T(8,128)S(1)} %get-tuple-element.9), channel_id=1, source_target_pairs={{0,32},{32,64},{64,96},{96,128},{128,160},{160,192},{192,224},{224... | collective-permute-start | bytes 368648 | tf_op jit(solution)/shard_map/ppermute | solution.py:16
  118.6 2.3 collective-permute-start.3
  120.9 1.5 fusion.20
  122.4 0.0 collective-permute-done.2
  122.4 3.2 %collective-permute-done.3 = f32[6,20,256]{2,1,0:T(8,128)S(1)} collective-permute-done((f32[6,20,256]{2,1,0:T(8,128)S(1)}, f32[6,20,256]{2,1,0:T(8,128)S(1)}, u32[]{:S(2)}, u32[]{:S(2)}) %collective-permute-start.3) | collective-permute-done | bytes 122912 | tf_op jit(solution)/shard_map/ppermute | solution.py:17
  125.6 0.0 copy-done.2
  125.6 0.0 copy-done.3
  125.6 1.5 fusion.19
  127.2 0.0 copy-start.1
  127.2 4.4 %collective-permute-start.4 = (f32[6,20,256]{2,1,0:T(8,128)S(1)}, f32[6,20,256]{2,1,0:T(8,128)S(1)}, u32[]{:S(2)}, u32[]{:S(2)}) collective-permute-start(f32[6,20,256]{2,1,0:T(8,128)S(1)} %get-tuple-element.7), channel_id=1, source_target_pairs={{0,32},{32,64},{64,96},{96,128},{128,160},{160,192},{192,224},{224... | collective-permute-start | bytes 368648 | tf_op jit(solution)/shard_map/ppermute | solution.py:16
  131.6 2.1 collective-permute-start.5
  133.7 1.5 fusion.22
  135.2 0.0 collective-permute-done.4
  135.2 4.6 %collective-permute-done.5 = f32[6,20,256]{2,1,0:T(8,128)S(1)} collective-permute-done((f32[6,20,256]{2,1,0:T(8,128)S(1)}, f32[6,20,256]{2,1,0:T(8,128)S(1)}, u32[]{:S(2)}, u32[]{:S(2)}) %collective-permute-start.5) | collective-permute-done | bytes 122912 | tf_op jit(solution)/shard_map/ppermute | solution.py:17
  139.9 1.5 fusion.44
  141.4 0.2 fusion.74
  141.6 0.0 copy-done.1
  141.6 1.9 collective-permute-start.6
  143.5 7.3 %collective-permute-start.7 = (f32[6,128,20]{2,1,0:T(8,128)S(1)}, f32[6,128,20]{2,1,0:T(8,128)S(1)}, u32[]{:S(2)}, u32[]{:S(2)}) collective-permute-start(f32[6,128,20]{2,1,0:T(8,128)S(1)} %get-tuple-element.6), channel_id=1, source_target_pairs={{1,0},{2,1},{3,2},{4,3},{5,4},{6,5},{7,6},{8,7},{9,8},{10,9},{11,1... | collective-permute-start | bytes 184328 | tf_op jit(solution)/shard_map/ppermute | solution.py:17
  150.8 0.0 copy-done.6
  150.8 1.5 fusion.23
  152.3 2.1 collective-permute-done.6
  154.4 1.7 collective-permute-done.7
  156.0 0.6 fusion.51
  156.6 1.6 fusion.14
  158.2 2.5 convolution_bitcast_fusion
  160.7 2.5 copy.45
  163.3 0.0 reduce-scatter.2.cloned.1.call-update
  163.3 0.0 copy-start.4
  164.1 0.0 copy-done.7
  164.1 0.6 fusion.70
  165.4 0.0 copy-done
  165.4 4.6 %fusion.30 = f32[32,6]{0,1:T(8,128)S(1)} fusion(f32[1,32,128,128]{3,2,0,1:T(8,128)S(1)} %copy-done, f32[6,128,2,128]{3,1,2,0:T(8,128)S(1)} %fusion.14, f32[32,2]{0,1:T(2,128)S(1)} %compare_convert_fusion), kind=kOutput, calls=%fused_computation.28 | convolution fusion | flops 75498048 | bytes 2884608 | tf_op jit(solution)/shard_map/krc,brjc->kbj/dot_general | solution.py:81
  170.1 0.1 copy.47
  170.2 134.2 %all-reduce.1 = f32[32,6]{1,0:T(8,128)S(1)} all-reduce(f32[32,6]{1,0:T(8,128)S(1)} %copy.47), channel_id=3, replica_groups=mesh['ty'=16,'tx'=32] {'tx'}, use_global_device_ids=true, to_apply=%region_4.0.clone | all-reduce | flops 192 | bytes 1536
  304.4 0.0 copy-done.4
  304.4 2.1 fusion.60
  307.2 1.2 maximum_bitcast_fusion
  (10 shorter events, 0.1 us)
Async XLA Ops:
  7.2 90.2 %all-gather.2.cloned.1.call-start = ((), (), s32[]{:S(2)}) async-start(), calls=%async_computation.1 | async-start | bytes 2162688 | tf_op jit(solution)/shard_map/all_gather | solution.py:51
  7.9 296.5 %reduce-scatter.2.cloned.1.call-start = ((), (), s32[]{:S(2)}) async-start(), calls=%async_computation.2 | async-start | bytes 2162688 | tf_op jit(solution)/shard_map/reduce_scatter | solution.py:84
  101.4 11.0 %copy-start.5 = (f32[6,41]{1,0:T(8,128)S(1)}, f32[6,41]{1,0:T(8,128)}, u32[]{:S(2)}) copy-start(f32[6,41]{1,0:T(8,128)} %param.14) | copy-start | bytes 2956
  101.8 10.8 %collective-permute-start = (f32[6,128,20]{1,2,0:T(8,128)S(1)}, f32[6,128,20]{1,2,0:T(8,128)S(1)}, u32[]{:S(2)}, u32[]{:S(2)}) collective-permute-start(f32[6,128,20]{1,2,0:T(8,128)S(1)} %get-tuple-element.13), channel_id=1, source_target_pairs={{0,1},{1,2},{2,3},{3,4},{4,5},{5,6},{6,7},{7,8},{8,9},{9,10},{10,1... | collective-permute-start | bytes 184328 | tf_op jit(solution)/shard_map/ppermute | solution.py:16
  103.9 9.0 %collective-permute-start.1 = (f32[6,128,20]{1,2,0:T(8,128)S(1)}, f32[6,128,20]{1,2,0:T(8,128)S(1)}, u32[]{:S(2)}, u32[]{:S(2)}) collective-permute-start(f32[6,128,20]{1,2,0:T(8,128)S(1)} %get-tuple-element.14), channel_id=1, source_target_pairs={{1,0},{2,1},{3,2},{4,3},{5,4},{6,5},{7,6},{8,7},{9,8},{10,9},{11,1... | collective-permute-start | bytes 184328 | tf_op jit(solution)/shard_map/ppermute | solution.py:17
  114.5 11.1 %copy-start.2 = (f32[6,128,256]{2,1,0:T(8,128)S(1)}, f32[6,128,256]{2,1,0:T(8,128)}, u32[]{:S(2)}) copy-start(f32[6,128,256]{2,1,0:T(8,128)} %param.9) | copy-start | bytes 2359300
  114.6 11.1 %copy-start.3 = (f32[6,128,256]{2,1,0:T(8,128)S(1)}, f32[6,128,256]{2,1,0:T(8,128)}, u32[]{:S(2)}) copy-start(f32[6,128,256]{2,1,0:T(8,128)} %param.8) | copy-start | bytes 2359300
  114.9 7.5 %collective-permute-start.2 = (f32[6,20,256]{2,1,0:T(8,128)S(1)}, f32[6,20,256]{2,1,0:T(8,128)S(1)}, u32[]{:S(2)}, u32[]{:S(2)}) collective-permute-start(f32[6,20,256]{2,1,0:T(8,128)S(1)} %get-tuple-element.9), channel_id=1, source_target_pairs={{0,32},{32,64},{64,96},{96,128},{128,160},{160,192},{192,224},{224... | collective-permute-start | bytes 368648 | tf_op jit(solution)/shard_map/ppermute | solution.py:16
  118.6 7.0 %collective-permute-start.3 = (f32[6,20,256]{2,1,0:T(8,128)S(1)}, f32[6,20,256]{2,1,0:T(8,128)S(1)}, u32[]{:S(2)}, u32[]{:S(2)}) collective-permute-start(f32[6,20,256]{2,1,0:T(8,128)S(1)} %get-tuple-element.10), channel_id=1, source_target_pairs={{32,0},{64,32},{96,64},{128,96},{160,128},{192,160},{224,192},{256... | collective-permute-start | bytes 368648 | tf_op jit(solution)/shard_map/ppermute | solution.py:17
  127.2 14.4 %copy-start.1 = (f32[6,128,256]{2,1,0:T(8,128)}, f32[6,128,256]{2,1,0:T(8,128)S(1)}, u32[]{:S(2)}) copy-start(f32[6,128,256]{2,1,0:T(8,128)S(1)} %fusion.19) | copy-start | bytes 2359300
  127.2 8.0 %collective-permute-start.4 = (f32[6,20,256]{2,1,0:T(8,128)S(1)}, f32[6,20,256]{2,1,0:T(8,128)S(1)}, u32[]{:S(2)}, u32[]{:S(2)}) collective-permute-start(f32[6,20,256]{2,1,0:T(8,128)S(1)} %get-tuple-element.7), channel_id=1, source_target_pairs={{0,32},{32,64},{64,96},{96,128},{128,160},{160,192},{192,224},{224... | collective-permute-start | bytes 368648 | tf_op jit(solution)/shard_map/ppermute | solution.py:16
  131.6 8.2 %collective-permute-start.5 = (f32[6,20,256]{2,1,0:T(8,128)S(1)}, f32[6,20,256]{2,1,0:T(8,128)S(1)}, u32[]{:S(2)}, u32[]{:S(2)}) collective-permute-start(f32[6,20,256]{2,1,0:T(8,128)S(1)} %get-tuple-element.8), channel_id=1, source_target_pairs={{32,0},{64,32},{96,64},{128,96},{160,128},{192,160},{224,192},{256... | collective-permute-start | bytes 368648 | tf_op jit(solution)/shard_map/ppermute | solution.py:17
  135.2 15.6 %copy-start.6 = (f32[6,41]{1,0:T(8,128)S(1)}, f32[6,41]{1,0:T(8,128)}, u32[]{:S(2)}) copy-start(f32[6,41]{1,0:T(8,128)} %param.15) | copy-start | bytes 2956
  141.6 12.8 %collective-permute-start.6 = (f32[6,128,20]{2,1,0:T(8,128)S(1)}, f32[6,128,20]{2,1,0:T(8,128)S(1)}, u32[]{:S(2)}, u32[]{:S(2)}) collective-permute-start(f32[6,128,20]{2,1,0:T(8,128)S(1)} %get-tuple-element.5), channel_id=1, source_target_pairs={{0,1},{1,2},{2,3},{3,4},{4,5},{5,6},{6,7},{7,8},{8,9},{9,10},{10,1... | collective-permute-start | bytes 184328 | tf_op jit(solution)/shard_map/ppermute | solution.py:16
  143.5 12.5 %collective-permute-start.7 = (f32[6,128,20]{2,1,0:T(8,128)S(1)}, f32[6,128,20]{2,1,0:T(8,128)S(1)}, u32[]{:S(2)}, u32[]{:S(2)}) collective-permute-start(f32[6,128,20]{2,1,0:T(8,128)S(1)} %get-tuple-element.6), channel_id=1, source_target_pairs={{1,0},{2,1},{3,2},{4,3},{5,4},{6,5},{7,6},{8,7},{9,8},{10,9},{11,1... | collective-permute-start | bytes 184328 | tf_op jit(solution)/shard_map/ppermute | solution.py:17
  163.3 0.8 copy-start.7
  163.3 2.1 copy-start
  163.3 141.1 %copy-start.4 = (f32[1,1,128,128]{3,2,1,0:T(8,128)S(1)}, f32[1,1,128,128]{3,2,1,0:T(8,128)}, u32[]{:S(2)}) copy-start(f32[1,1,128,128]{3,2,1,0:T(8,128)} %param.11) | copy-start | bytes 196612
Sparse Core Ops, SparseCore 0:
  11.3 86.0 all-gather.1
  163.4 126.2 reduce-scatter.1
where the time goes:
time: 316 us; the launch traced here: 315 us
  blocking collectives  188 us (59%)
  waiting for transfers between devices  45.2 us (14%)
  starting transfers between devices  30.9 us (10%)
  matrix products  23.3 us (7%)
  between operations  17.1 us (5%)
  local copies, waits for them, and re-layouts  6.49 us (2%)
  other arithmetic  4.64 us (1%)
    unnamed x2, blocking collectives  148 us
    all_gather x1, blocking collectives, body(): lax.all_gather(sed, 'tx', axis=1, tiled=True)  39.6 us
    all_gather x1, waiting for transfers between devices, body(): lax.all_gather(morph, 'tx', axis=1, tiled=True)  32.4 us
    ppermute x4, starting transfers between devices, with_halo(): after = lax.ppermute(leading, axis, down)  18.7 us
    ppermute x4, starting transfers between devices, with_halo(): before = lax.ppermute(last, axis, up)  12.1 us
    ppermute x4, waiting for transfers between devices, with_halo(): after = lax.ppermute(leading, axis, down)  9.93 us
  transfers between devices with their start and end apart: 10, of which 6 were waited for; matrix products, arithmetic and copies ran while one was open for 5% of the time, Pallas kernels for 0%

commit v1 on v0

--- a/solution.py
+++ b/solution.py
@@ -48,7 +48,9 @@
     rim_width = (row_kernel.shape[1] - 1) // 2
     all_sed, all_morph, all_foot = (
         lax.all_gather(sed, "tx", axis=1, tiled=True),
-        lax.all_gather(morph, "tx", axis=1, tiled=True),
+        jnp.concatenate(
+            lax.all_to_all(jnp.stack([morph] * lax.axis_size("tx")), "tx", 0, 0), axis=1
+        ),
         lax.all_gather(foot_block, "tx", axis=1, tiled=True),
     )
     all_sed = all_sed[0]

time: 316 us -> 342 us (1.082)
  the two profiles are of different devices: /device:TPU:96 before, /device:TPU:34 now
where the time goes in v1:
time: 342 us; the launch traced here: 341 us
  blocking collectives  227 us (66%)
  starting transfers between devices  49.9 us (15%)
  matrix products  23.8 us (7%)
  between operations  17 us (5%)
  local copies, waits for them, and re-layouts  10.4 us (3%)
  waiting for transfers between devices  7.5 us (2%)
  other arithmetic  5.72 us (2%)
    unnamed x2, blocking collectives  150 us
    all_gather x1, blocking collectives, body(): lax.all_gather(sed, 'tx', axis=1, tiled=True)  77.3 us
    ppermute x4, starting transfers between devices, with_halo(): after = lax.ppermute(leading, axis, down)  30.7 us
    ppermute x4, starting transfers between devices, with_halo(): before = lax.ppermute(last, axis, up)  10.2 us
    all_to_all x1, starting transfers between devices, body(): lax.all_to_all(jnp.stack([morph] * lax.axis_size('tx')), 'tx', 0, 0)  9.06 us
  transfers between devices with their start and end apart: 10, of which 6 were waited for; matrix products, arithmetic and copies ran while one was open for 4% of the time, Pallas kernels for 0%

profile of v1, /device:TPU:34, one launch (start us, length us, event | category | flops | bytes accessed | tf_op | source)
XLA Modules:
  0.0 341.4 jit_solution(16911249605065898569)
XLA Ops:
  7.2 2.4 stack.14
  9.6 0.0 copy-start.4
  9.6 9.1 %all-to-all-start = ((f32[32,1,1,128,128]{4,3,2,1,0:T(8,128)}), f32[32,1,1,128,128]{4,3,2,1,0:T(8,128)S(1)}, u32[]{:S(2)}, u32[]{:S(2)}) async-start(f32[32,1,1,128,128]{4,3,2,1,0:T(8,128)} %stack.14), calls=%async_computation | async-start | bytes 4194304 | tf_op jit(solution)/shard_map/all_to_all | solution.py:52
  18.7 0.0 reduce-scatter.2.cloned.1.call-start
  19.4 0.0 copy-done.4
  19.4 0.1 rev.7
  19.4 0.0 copy-done.5
  19.4 77.3 %all_gather.7 = f32[1,32,6]{2,0,1:T(1,128)S(1)} all-gather(f32[1,1,6]{2,0,1:T(1,128)S(1)} %bitcast.109), channel_id=1, replica_groups=mesh['ty'=16,'tx'=32] {'tx'}, dimensions={1}, use_global_device_ids=true | all-gather | bytes 792 | tf_op jit(solution)/shard_map/all_gather | solution.py:50
  96.8 0.1 copy.30
  96.8 0.0 copy-done.6
  96.9 0.6 fusion.78
  97.5 0.7 bitcast_dynamic-update-slice_fusion
  98.2 15.6 %all-reduce = s32[32]{0:T(128)S(1)} all-reduce(s32[32]{0:T(128)S(1)} %bitcast_dynamic-update-slice_fusion), channel_id=1, replica_groups=mesh['ty'=16,'tx'=32] {'tx'}, use_global_device_ids=true, to_apply=%add | all-reduce | flops 32 | bytes 256
  113.7 0.1 compare_convert_fusion
  113.8 0.0 all-to-all-done
  113.8 2.5 fusion.16
  116.3 0.0 copy-start.3
  116.3 1.2 copy.32
  117.5 0.9 fusion.77
  118.4 1.9 collective-permute-start
  120.4 7.3 %collective-permute-start.1 = (f32[6,128,20]{1,2,0:T(8,128)S(1)}, f32[6,128,20]{1,2,0:T(8,128)S(1)}, u32[]{:S(2)}, u32[]{:S(2)}) collective-permute-start(f32[6,128,20]{1,2,0:T(8,128)S(1)} %get-tuple-element.14), channel_id=1, source_target_pairs={{1,0},{2,1},{3,2},{4,3},{5,4},{6,5},{7,6},{8,7},{9,8},{10,9},{11,1... | collective-permute-start | bytes 184328 | tf_op jit(solution)/shard_map/ppermute | solution.py:17
  127.6 1.5 fusion.21
  129.1 0.0 copy-done.3
  129.1 0.1 rev.6
  129.2 0.0 collective-permute-done
  129.2 0.4 collective-permute-done.1
  129.6 1.2 fusion.53
  130.8 2.4 fusion.35
  133.2 1.4 copy.34
  134.6 0.0 copy-start.1
  134.7 4.4 %collective-permute-start.2 = (f32[6,20,256]{2,1,0:T(8,128)S(1)}, f32[6,20,256]{2,1,0:T(8,128)S(1)}, u32[]{:S(2)}, u32[]{:S(2)}) collective-permute-start(f32[6,20,256]{2,1,0:T(8,128)S(1)} %get-tuple-element.9), channel_id=1, source_target_pairs={{0,32},{32,64},{64,96},{96,128},{128,160},{160,192},{192,224},{224... | collective-permute-start | bytes 368648 | tf_op jit(solution)/shard_map/ppermute | solution.py:16
  139.1 9.5 %collective-permute-start.3 = (f32[6,20,256]{2,1,0:T(8,128)S(1)}, f32[6,20,256]{2,1,0:T(8,128)S(1)}, u32[]{:S(2)}, u32[]{:S(2)}) collective-permute-start(f32[6,20,256]{2,1,0:T(8,128)S(1)} %get-tuple-element.10), channel_id=1, source_target_pairs={{32,0},{64,32},{96,64},{128,96},{160,128},{192,160},{224,192},{256... | collective-permute-start | bytes 368648 | tf_op jit(solution)/shard_map/ppermute | solution.py:17
  148.6 1.5 fusion.20
  150.1 1.0 collective-permute-done.2
  151.0 1.2 collective-permute-done.3
  152.2 0.0 copy-done.1
  152.2 2.7 fusion.19
  154.9 0.0 copy-start
  155.0 1.9 collective-permute-start.4
  156.9 6.7 %collective-permute-start.5 = (f32[6,20,256]{2,1,0:T(8,128)S(1)}, f32[6,20,256]{2,1,0:T(8,128)S(1)}, u32[]{:S(2)}, u32[]{:S(2)}) collective-permute-start(f32[6,20,256]{2,1,0:T(8,128)S(1)} %get-tuple-element.8), channel_id=1, source_target_pairs={{32,0},{64,32},{96,64},{128,96},{160,128},{192,160},{224,192},{256... | collective-permute-start | bytes 368648 | tf_op jit(solution)/shard_map/ppermute | solution.py:17
  163.6 1.5 fusion.22
  165.1 0.0 collective-permute-done.4
  165.1 1.1 collective-permute-done.5
  166.2 1.5 fusion.44
  167.7 0.2 fusion.74
  167.9 0.0 copy-done
  167.9 1.9 collective-permute-start.6
  169.8 7.3 %collective-permute-start.7 = (f32[6,128,20]{2,1,0:T(8,128)S(1)}, f32[6,128,20]{2,1,0:T(8,128)S(1)}, u32[]{:S(2)}, u32[]{:S(2)}) collective-permute-start(f32[6,128,20]{2,1,0:T(8,128)S(1)} %get-tuple-element.6), channel_id=1, source_target_pairs={{1,0},{2,1},{3,2},{4,3},{5,4},{6,5},{7,6},{8,7},{9,8},{10,9},{11,1... | collective-permute-start | bytes 184328 | tf_op jit(solution)/shard_map/ppermute | solution.py:17
  177.1 1.5 fusion.23
  178.6 2.1 collective-permute-done.6
  180.7 1.7 collective-permute-done.7
  182.4 0.6 fusion.51
  183.0 1.6 fusion.14
  184.5 2.5 convolution_bitcast_fusion
  187.1 2.6 copy.42
  189.6 0.0 reduce-scatter.2.cloned.1.call-update
  189.6 0.0 copy-start.2
  190.3 0.6 fusion.70
  191.6 4.6 %fusion.30 = f32[32,6]{0,1:T(8,128)S(1)} fusion(f32[32,1,1,128,128]{4,3,2,1,0:T(8,128)S(1)} %all-to-all-done, f32[6,128,2,128]{3,1,2,0:T(8,128)S(1)} %fusion.14, f32[32,2]{0,1:T(2,128)S(1)} %compare_convert_fusion), kind=kOutput, calls=%fused_computation.28 | convolution fusion | flops 75498048 | bytes 2884608 | tf_op jit(solution)/shard_map/krc,brjc->kbj/dot_general | solution.py:83
  196.3 0.1 copy.44
  196.4 134.2 %all-reduce.1 = f32[32,6]{1,0:T(8,128)S(1)} all-reduce(f32[32,6]{1,0:T(8,128)S(1)} %copy.44), channel_id=3, replica_groups=mesh['ty'=16,'tx'=32] {'tx'}, use_global_device_ids=true, to_apply=%region_4.0.clone | all-reduce | flops 192 | bytes 1536
  330.6 0.0 copy-done.2
  330.6 2.1 fusion.60
  333.4 1.1 maximum_bitcast_fusion
  (8 shorter events, 0.1 us)
Async XLA Ops:
  9.6 9.8 %copy-start.4 = (f32[6,41]{1,0:T(8,128)S(1)}, f32[6,41]{1,0:T(8,128)}, u32[]{:S(2)}) copy-start(f32[6,41]{1,0:T(8,128)} %param.15) | copy-start | bytes 2956
  9.6 9.9 %copy-start.5 = (f32[1,1,6]{2,1,0:T(1,128)S(1)}, f32[1,1,6]{2,1,0:T(1,128)}, u32[]{:S(2)}) copy-start(f32[1,1,6]{2,1,0:T(1,128)} %param.10) | copy-start | bytes 76
  9.6 87.3 %copy-start.6 = (u32[512]{0:T(512)S(1)}, u32[512]{0:T(512)}, u32[]{:S(2)}) copy-start(u32[512]{0:T(512)} %constant.16) | copy-start | bytes 6148
  9.6 104.2 %all-to-all-start = ((f32[32,1,1,128,128]{4,3,2,1,0:T(8,128)}), f32[32,1,1,128,128]{4,3,2,1,0:T(8,128)S(1)}, u32[]{:S(2)}, u32[]{:S(2)}) async-start(f32[32,1,1,128,128]{4,3,2,1,0:T(8,128)} %stack.14), calls=%async_computation | async-start | bytes 4194304 | tf_op jit(solution)/shard_map/all_to_all | solution.py:52
  18.7 312.0 %reduce-scatter.2.cloned.1.call-start = ((), (), s32[]{:S(2)}) async-start(), calls=%async_computation.2 | async-start | bytes 2162688 | tf_op jit(solution)/shard_map/reduce_scatter | solution.py:86
  116.3 12.8 %copy-start.3 = (f32[6,41]{1,0:T(8,128)S(1)}, f32[6,41]{1,0:T(8,128)}, u32[]{:S(2)}) copy-start(f32[6,41]{1,0:T(8,128)} %param.14) | copy-start | bytes 2956
  118.4 10.8 %collective-permute-start = (f32[6,128,20]{1,2,0:T(8,128)S(1)}, f32[6,128,20]{1,2,0:T(8,128)S(1)}, u32[]{:S(2)}, u32[]{:S(2)}) collective-permute-start(f32[6,128,20]{1,2,0:T(8,128)S(1)} %get-tuple-element.13), channel_id=1, source_target_pairs={{0,1},{1,2},{2,3},{3,4},{4,5},{5,6},{6,7},{7,8},{8,9},{9,10},{10,1... | collective-permute-start | bytes 184328 | tf_op jit(solution)/shard_map/ppermute | solution.py:16
  120.4 9.2 %collective-permute-start.1 = (f32[6,128,20]{1,2,0:T(8,128)S(1)}, f32[6,128,20]{1,2,0:T(8,128)S(1)}, u32[]{:S(2)}, u32[]{:S(2)}) collective-permute-start(f32[6,128,20]{1,2,0:T(8,128)S(1)} %get-tuple-element.14), channel_id=1, source_target_pairs={{1,0},{2,1},{3,2},{4,3},{5,4},{6,5},{7,6},{8,7},{9,8},{10,9},{11,1... | collective-permute-start | bytes 184328 | tf_op jit(solution)/shard_map/ppermute | solution.py:17
  134.6 17.6 %copy-start.1 = (f32[6,128,256]{2,1,0:T(8,128)S(1)}, f32[6,128,256]{2,1,0:T(8,128)}, u32[]{:S(2)}) copy-start(f32[6,128,256]{2,1,0:T(8,128)} %param.9) | copy-start | bytes 2359300
  134.7 16.4 %collective-permute-start.2 = (f32[6,20,256]{2,1,0:T(8,128)S(1)}, f32[6,20,256]{2,1,0:T(8,128)S(1)}, u32[]{:S(2)}, u32[]{:S(2)}) collective-permute-start(f32[6,20,256]{2,1,0:T(8,128)S(1)} %get-tuple-element.9), channel_id=1, source_target_pairs={{0,32},{32,64},{64,96},{96,128},{128,160},{160,192},{192,224},{224... | collective-permute-start | bytes 368648 | tf_op jit(solution)/shard_map/ppermute | solution.py:16
  139.1 13.1 %collective-permute-start.3 = (f32[6,20,256]{2,1,0:T(8,128)S(1)}, f32[6,20,256]{2,1,0:T(8,128)S(1)}, u32[]{:S(2)}, u32[]{:S(2)}) collective-permute-start(f32[6,20,256]{2,1,0:T(8,128)S(1)} %get-tuple-element.10), channel_id=1, source_target_pairs={{32,0},{64,32},{96,64},{128,96},{160,128},{192,160},{224,192},{256... | collective-permute-start | bytes 368648 | tf_op jit(solution)/shard_map/ppermute | solution.py:17
  154.9 13.0 %copy-start = (f32[6,128,256]{2,1,0:T(8,128)}, f32[6,128,256]{2,1,0:T(8,128)S(1)}, u32[]{:S(2)}) copy-start(f32[6,128,256]{2,1,0:T(8,128)S(1)} %fusion.19) | copy-start | bytes 2359300
  155.0 10.1 %collective-permute-start.4 = (f32[6,20,256]{2,1,0:T(8,128)S(1)}, f32[6,20,256]{2,1,0:T(8,128)S(1)}, u32[]{:S(2)}, u32[]{:S(2)}) collective-permute-start(f32[6,20,256]{2,1,0:T(8,128)S(1)} %get-tuple-element.7), channel_id=1, source_target_pairs={{0,32},{32,64},{64,96},{96,128},{128,160},{160,192},{192,224},{224... | collective-permute-start | bytes 368648 | tf_op jit(solution)/shard_map/ppermute | solution.py:16
  156.9 9.3 %collective-permute-start.5 = (f32[6,20,256]{2,1,0:T(8,128)S(1)}, f32[6,20,256]{2,1,0:T(8,128)S(1)}, u32[]{:S(2)}, u32[]{:S(2)}) collective-permute-start(f32[6,20,256]{2,1,0:T(8,128)S(1)} %get-tuple-element.8), channel_id=1, source_target_pairs={{32,0},{64,32},{96,64},{128,96},{160,128},{192,160},{224,192},{256... | collective-permute-start | bytes 368648 | tf_op jit(solution)/shard_map/ppermute | solution.py:17
  167.9 12.8 %collective-permute-start.6 = (f32[6,128,20]{2,1,0:T(8,128)S(1)}, f32[6,128,20]{2,1,0:T(8,128)S(1)}, u32[]{:S(2)}, u32[]{:S(2)}) collective-permute-start(f32[6,128,20]{2,1,0:T(8,128)S(1)} %get-tuple-element.5), channel_id=1, source_target_pairs={{0,1},{1,2},{2,3},{3,4},{4,5},{5,6},{6,7},{7,8},{8,9},{9,10},{10,1... | collective-permute-start | bytes 184328 | tf_op jit(solution)/shard_map/ppermute | solution.py:16
  169.8 12.5 %collective-permute-start.7 = (f32[6,128,20]{2,1,0:T(8,128)S(1)}, f32[6,128,20]{2,1,0:T(8,128)S(1)}, u32[]{:S(2)}, u32[]{:S(2)}) collective-permute-start(f32[6,128,20]{2,1,0:T(8,128)S(1)} %get-tuple-element.6), channel_id=1, source_target_pairs={{1,0},{2,1},{3,2},{4,3},{5,4},{6,5},{7,6},{8,7},{9,8},{10,9},{11,1... | collective-permute-start | bytes 184328 | tf_op jit(solution)/shard_map/ppermute | solution.py:17
  189.6 141.0 %copy-start.2 = (f32[1,1,128,128]{3,2,1,0:T(8,128)S(1)}, f32[1,1,128,128]{3,2,1,0:T(8,128)}, u32[]{:S(2)}) copy-start(f32[1,1,128,128]{3,2,1,0:T(8,128)} %param.11) | copy-start | bytes 196612
Sparse Core Ops, SparseCore 0:
  189.8 126.1 reduce-scatter.1
